TPU v7x, 32 devices: a whole 2x2x4 slice. The times are simulated.
32 devices in a mesh: row: 8 (over y, x, core), col: 4 (over z).
Axes of the slice: x: 2, y: 2, z: 4, core: 2. Of those that a mesh axis runs over, the one named last changes fastest.
Arguments:
- right_sides: float32 [64, 32768], P(None, ('row', 'col'))
- diag_tiles: float32 [32, 1024, 1024], P(('row', 'col')), as said below
- low_rank: float32 [32, 4, 8, 2, 12, 1024], P('row', 'col'), as said below
- tile_ranks: int32 [32, 4, 8], P('row', 'col'), may hold values from 1 to 12, as said below
- inv_factor: float32 [256, 8, 128, 128], P(('row', 'col')), as said below
- sub_sizes: int32 [64], replicated, may hold values from 1 to 8, 256 in all
Outputs:
- solution: float32 [64, 32768], P(None, ('row', 'col'))
- residual: float32 [64, 32768], P(None, ('row', 'col'))
Inputs may be any that keep to these rules, and one draw needn't show every extreme that they name: `low_rank`: tile (j, i) holds the two factors of tile (i, j) in swapped order, and a diagonal tile's two factors are equal, so S is symmetric. `tile_ranks`: the rank of tile (i, j) equals that of tile (j, i); diagonal tiles have rank 12. `diag_tiles`: each tile is symmetric positive definite. `inv_factor`: the block at distance 0 of every span is lower triangular with a positive diagonal. `sub_sizes`: the sizes sum to 256.
All inputs are finite; a program needn't handle non-finite values.
Results may differ from a plain program's by a relative error of at most 0.0003.
Values sent between devices are 32-bit elements; how exact they have to be, the bound alone decides.
A program may use at most 128 MiB of HBM per device.

v0:
```python
import functools
import math

import jax
import jax.numpy as jnp
from jax import lax
from jax.experimental import pallas as pl
from jax.experimental.pallas import tpu as pltpu
from jax.sharding import PartitionSpec as P

MESH = pl.DeviceIdType.MESH
F32 = jnp.float32
BF16 = jnp.bfloat16
LOW = 8
LANES = 128


def split(x):
    high = x.astype(BF16)
    return high, (x - high.astype(F32)).astype(BF16)


def stacked(x):
    high, low = split(x)
    return jnp.concatenate([high, low], axis=0)


def dot_nt(a, b):
    return lax.dot_general(a, b, (((1,), (1,)), ((), ())), preferred_element_type=F32)


def dot_nn(a, b):
    return lax.dot_general(a, b, (((1,), (0,)), ((), ())), preferred_element_type=F32)


def product3(dot, both, high, low):
    rows = both.shape[0] // 2
    first = dot(both, high)
    return first[:rows] + (first[rows:] + dot(both[:rows], low))


def gram(a, b):
    return lax.dot_general(
        a, b, (((1,), (1,)), ((), ())), precision=lax.Precision.HIGHEST, preferred_element_type=F32
    )


def mixed(coeffs, rows):
    return jnp.dot(coeffs, rows, precision=lax.Precision.HIGHEST, preferred_element_type=F32)


def eliminate(work):
    count, width = work.shape
    block = 4
    row_ids = lax.broadcasted_iota(jnp.int32, work.shape, 0)
    for k in range(0, count, block):
        columns = [jnp.broadcast_to(work[:, k + j : k + j + 1], work.shape) for j in range(block)]
        rows = [work[k + i : k + i + 1, :] for i in range(block)]
        heads = [[columns[j][k + i : k + i + 1, :] for j in range(block)] for i in range(block)]
        for i in range(block):
            inverse = 1.0 / heads[i][i]
            rows[i] = rows[i] * inverse
            for j in range(i + 1, block):
                heads[i][j] = heads[i][j] * inverse
            for other in range(block):
                if other != i:
                    factor = heads[other][i]
                    rows[other] = rows[other] - factor * rows[i]
                    for j in range(i + 1, block):
                        heads[other][j] = heads[other][j] - factor * heads[i][j]
        update = columns[0] * rows[0]
        for j in range(1, block):
            update = update + columns[j] * rows[j]
        work = work - update
        for i in range(block):
            work = jnp.where(row_ids == k + i, rows[i], work)
    return work


def solved(work):
    return eliminate(work).T[work.shape[0] :, :]


def kernel(
    rows, cols,
    x_ref, diag_ref, factor_ref, ranks_ref, inv_ref, sizes_ref,
    sol_ref, res_ref,
    inv_f32, inv_hi, inv_lo, diag_f32, diag_hi, diag_lo, u_f32, u_hi, u_lo,
    factor_f32, packed, joined, halo_in, back_out, back_in, spread, vec_z, vec_q, coef_out, coef_in, sum_row, sum_col,
    inv_sem, diag_sem, factor_sem, own_sem, u_send, u_recv, halo_send, halo_recv, back_send, back_recv,
    coef_send, coef_recv, row_send, row_recv, col_send, col_recv,
):
    my_row, my_col = lax.axis_index("row"), lax.axis_index("col")
    total = rows * cols
    me = my_row * cols + my_col
    rhs, tile = x_ref.shape
    spans, reach, span, _ = inv_ref.shape
    halo = (reach - 1) * span
    wide = reach * span

    def coords(device):
        return (device // cols, device % cols)

    following = coords((me + 1) % total)
    previous = coords((me + total - 1) % total)

    barrier = pltpu.get_barrier_semaphore()

    def greet(step, carry):
        pl.semaphore_signal(
            barrier, inc=1, device_id=coords((me + step) % total), device_id_type=MESH
        )
        return carry

    lax.fori_loop(1, total, greet, 0)

    factor_copy = pltpu.make_async_copy(factor_ref, factor_f32, factor_sem)
    factor_copy.start()
    for a in range(spans):
        for t in range(reach):
            copy = pltpu.make_async_copy(
                inv_ref.at[a, t],
                inv_f32.at[a, :, (reach - 1 - t) * span : (reach - t) * span],
                inv_sem.at[a],
            )
            copy.start()
    diag_copy = pltpu.make_async_copy(diag_ref.at[0], diag_f32, diag_sem)
    diag_copy.start()
    groups = rows
    rank = factor_ref.shape[0] // (cols * groups * 2 * (tile // LANES))
    tail = rank - LOW
    step_rows = 2 * (tile // LANES)

    def at_rows(ref, index, size):
        return ref.at[pl.ds(pl.multiple_of(index * size, size), size), :]

    def take(base, side, first, size, limit):
        ids = first + lax.broadcasted_iota(jnp.int32, (size, LANES), 0)
        pieces = [
            factor_f32[pl.ds(base + first * step_rows + 2 * i + side, size, stride=step_rows), :]
            for i in range(tile // LANES)
        ]
        return jnp.concatenate([jnp.where(ids < limit, piece, 0.0) for piece in pieces], axis=1)

    factor_copy.wait()

    def block(base, side, limit):
        rest = take(base, side, LOW, tail, limit)
        rest = jnp.concatenate([rest[:, : tile // 2], rest[:, tile // 2 :]], axis=0)
        return take(base, side, 0, LOW, limit), rest

    def pack(k, carry):
        for a in range(cols):
            base = (a * groups + k) * rank * step_rows
            first, rest = block(base, 1, ranks_ref[a, 0, k])
            packed[k, a * LOW : (a + 1) * LOW, :tile] = first
            packed[k, a * LOW : (a + 1) * LOW, tile:] = rest
        base = (my_col * groups + k) * rank * step_rows
        where = pl.ds(pl.multiple_of((k * cols + my_col) * LOW, LOW), LOW)
        first, rest = block(base, 0, ranks_ref[my_col, 0, k])
        u_f32[where, :tile] = first
        u_f32[where, tile:] = rest
        return carry

    lax.fori_loop(0, groups, pack, 0)

    for turn in range(1, cols):
        a = (my_col + turn) % cols
        pltpu.make_async_copy(
            at_rows(packed.at[my_row], a, LOW), at_rows(u_f32, my_row * cols + a, LOW), own_sem.at[1]
        ).start()
    pl.semaphore_wait(barrier, total - 1)

    def remote(src, dst, send, recv, device):
        return pltpu.make_async_remote_copy(
            src_ref=src, dst_ref=dst, send_sem=send, recv_sem=recv, device_id=device,
            device_id_type=MESH,
        )

    def halo_copy(src, call):
        return remote(
            src.at[:, tile - halo : tile], halo_in.at[call], halo_send.at[call],
            halo_recv.at[call], following,
        )

    first_halo = halo_copy(x_ref, 0)
    first_halo.start()

    def send_factors(step, carry):
        peer = (my_row + step) % rows
        for turn in range(1, cols):
            a = (my_col + turn) % cols
            remote(at_rows(packed.at[peer], a, LOW), at_rows(u_f32, my_row * cols + a, LOW),
                   u_send, u_recv, (peer, my_col)).start()
        return carry

    lax.fori_loop(1, rows, send_factors, 0)

    subs = sizes_ref.shape[1]
    sizes = jnp.broadcast_to(sizes_ref[...].astype(F32), (subs, subs))
    down = lax.broadcasted_iota(jnp.int32, (subs, subs), 0)
    across = lax.broadcasted_iota(jnp.int32, (subs, subs), 1)
    opening = jnp.sum(jnp.where(across < down, sizes, 0.0), axis=1, keepdims=True)
    behind = (reach - 1) - lax.broadcasted_iota(jnp.int32, (1, wide), 1) // span
    behind = behind.astype(F32)

    vec = x_ref[...]
    joined[:, halo:] = stacked(vec)

    for a in range(spans):
        for t in range(reach):
            pltpu.make_async_copy(
                inv_ref.at[a, t], inv_f32.at[a, :, t * span : (t + 1) * span], inv_sem.at[a]
            ).wait()
        number = (me * spans + a).astype(F32)
        start = jnp.max(jnp.where(opening <= number, opening, 0.0), axis=0, keepdims=True)
        mask = jnp.where(behind <= number - start, 1.0, 0.0)
        high, low = split(inv_f32[a] * mask)
        inv_hi[a] = high
        inv_lo[a] = low

    def forward_own():
        parts = []
        for a in range(spans):
            skip = max(0, halo - a * span)
            parts.append(product3(
                dot_nt, joined[:, a * span + skip : a * span + wide],
                inv_hi[a, :, skip:], inv_lo[a, :, skip:],
            ))
        return parts

    def forward_halo(parts, call):
        joined[:, :halo] = stacked(halo_in[call])
        out = []
        for a in range(spans):
            skip = max(0, halo - a * span)
            part = parts[a]
            if skip:
                part = part + product3(
                    dot_nt, joined[:, a * span : halo], inv_hi[a, :, :skip], inv_lo[a, :, :skip]
                )
            out.append(stacked(part))
        return out

    def backward_halo(forward, call):
        spread[:, :halo] = jnp.zeros((rhs, halo), F32)
        for a in range(spans):
            skip = max(0, halo - a * span)
            if skip:
                spread[:, a * span : halo] += product3(
                    dot_nn, forward[a], inv_hi[a, :, :skip], inv_lo[a, :, :skip]
                )
        back_out[call] = spread[:, :halo]
        copy = remote(back_out.at[call], back_in.at[call], back_send.at[call],
                      back_recv.at[call], previous)
        copy.start()
        return copy

    def backward_own(forward):
        spread[:, halo:] = jnp.zeros((rhs, tile), F32)
        for a in range(spans):
            skip = max(0, halo - a * span)
            spread[:, a * span + skip : a * span + wide] += product3(
                dot_nn, forward[a], inv_hi[a, :, skip:], inv_lo[a, :, skip:]
            )

    def returned(call):
        spread[:, halo + tile - halo :] += back_in[call]
        return spread[:, halo:]

    def send_coeffs(both, call):
        wide_part = dot_nt(u_hi[...], both)
        coeffs = wide_part[:, :rhs] + (wide_part[:, rhs:] + dot_nt(u_lo[...], both[:rhs]))
        half = coeffs.shape[0] // 2
        coef_out[call, :, :rhs] = coeffs[:half]
        coef_out[call, :, rhs:] = coeffs[half:]

        def send(peer_row, peer_col):
            remote(at_rows(coef_out.at[call], peer_row * cols + peer_col, LOW),
                   at_rows(coef_in.at[call], me, LOW),
                   coef_send.at[call], coef_recv.at[call], (peer_row, peer_col)).start()

        def send_row(step, carry):
            peer_row = (my_row + step) % rows
            for turn in range(cols):
                send(peer_row, (my_col + turn) % cols)
            return carry

        lax.fori_loop(1, rows, send_row, 0)
        for turn in range(1, cols):
            send(my_row, (my_col + turn) % cols)
        pltpu.make_async_copy(
            at_rows(coef_out.at[call], me, LOW), at_rows(coef_in.at[call], me, LOW), own_sem.at[2 + call]
        ).start()

    def wait_coeffs(call):
        piece = coef_out.at[call, : (total - 1) * LOW, :]
        pltpu.make_async_copy(piece, piece, coef_recv.at[call]).wait()
        pltpu.make_async_copy(
            at_rows(coef_out.at[call], me, LOW), at_rows(coef_in.at[call], me, LOW), own_sem.at[2 + call]
        ).wait()
        turned = coef_in[call].T
        return stacked(jnp.concatenate([turned[:rhs], turned[rhs:]], axis=1))

    def far_part(call):
        return product3(dot_nn, wait_coeffs(call), u_hi[...], u_lo[...])

    heights = (rhs // 2, rhs, rhs // 2, rhs // 2)

    def start_sum(value, call):
        high = heights[call]
        sum_row[call, my_row, :high] = value
        for step in range(1, rows):
            mine = sum_row.at[call, my_row, :high]
            remote(mine, mine, row_send.at[call],
                   row_recv.at[call], ((my_row + step) % rows, my_col)).start()

    def middle_sum(call):
        high = heights[call]
        piece = sum_row.at[call, : rows - 1, :high]
        pltpu.make_async_copy(piece, piece, row_recv.at[call]).wait()
        sum_col[call, my_col, :high] = jnp.sum(sum_row[call, :, :high], axis=0)
        for step in range(1, cols):
            mine = sum_col.at[call, my_col, :high]
            remote(mine, mine, col_send.at[call],
                   col_recv.at[call], (my_row, (my_col + step) % cols)).start()

    def end_sum(call):
        high = heights[call]
        piece = sum_col.at[call, : cols - 1, :high]
        pltpu.make_async_copy(piece, piece, col_recv.at[call]).wait()
        return jnp.sum(sum_col[call, :, :high], axis=0)

    def folded(square):
        return jnp.concatenate([square[: rhs // 2], square[rhs // 2 :]], axis=1)

    def unfolded(halves):
        return jnp.concatenate([halves[:, :rhs], halves[:, rhs:]], axis=0)

    parts = forward_own()
    first_halo.wait_recv()
    forward = forward_halo(parts, 0)
    first_back = backward_halo(forward, 0)
    backward_own(forward)
    diag_copy.wait()

    def split_diag(step, carry):
        where = pl.ds(pl.multiple_of(step * span, span), span)
        high, low = split(diag_f32[where, :])
        diag_hi[where, :] = high
        diag_lo[where, :] = low
        return carry

    lax.fori_loop(0, tile // span, split_diag, 0)
    own_piece = u_f32.at[: (cols - 1) * LOW, :]
    pltpu.make_async_copy(own_piece, own_piece, own_sem.at[1]).wait()
    others = u_f32.at[: (rows - 1) * (cols - 1) * LOW, :]
    pltpu.make_async_copy(others, others, u_recv).wait()
    empty = jnp.zeros((LOW - tail, tile), F32)

    def split_factors(step, carry):
        where = pl.ds(pl.multiple_of(step * 2 * LOW, 2 * LOW), 2 * LOW)
        high, low = split(u_f32[where, :tile])
        u_hi[where, :] = high
        u_lo[where, :] = low
        rest = u_f32[where, tile:]
        parts = []
        for first in (0, LOW):
            parts.append(jnp.concatenate(
                [rest[first : first + tail], rest[first + tail : first + 2 * tail]], axis=1
            ))
            parts.append(empty)
        high, low = split(jnp.concatenate(parts, axis=0))
        later = pl.ds(pl.multiple_of(total * LOW + step * 2 * LOW, 2 * LOW), 2 * LOW)
        u_hi[later, :] = high
        u_lo[later, :] = low
        return carry

    lax.fori_loop(0, total // 2, split_factors, 0)
    first_back.wait_recv()
    z0 = returned(0)
    vec_z[...] = z0

    both = stacked(z0)
    send_coeffs(both, 0)
    start_sum(folded(gram(z0, x_ref[...])), 3)
    near = product3(dot_nn, both, diag_hi[...], diag_lo[...])
    middle_sum(3)
    q0 = near + far_part(0)
    vec_q[...] = q0
    second_halo = halo_copy(vec_q, 1)
    second_halo.start()

    start_sum(folded(gram(z0, q0)), 0)
    joined[:, halo:] = stacked(q0)
    parts = forward_own()
    middle_sum(0)
    second_halo.wait_recv()
    forward = forward_halo(parts, 1)
    second_back = backward_halo(forward, 1)
    backward_own(forward)
    rho0 = unfolded(end_sum(3))
    curve = unfolded(end_sum(0))
    alpha0 = solved(jnp.concatenate([curve, rho0], axis=1))
    res1 = x_ref[...] - mixed(alpha0, vec_q[...])
    second_back.wait_recv()
    z1 = vec_z[...] - mixed(alpha0, returned(1))

    both = stacked(z1)
    send_coeffs(both, 1)
    start_sum(jnp.concatenate([gram(vec_q[...], z1), gram(z1, res1)], axis=1), 1)
    near = product3(dot_nn, both, diag_hi[...], diag_lo[...])
    square = (rhs, rhs)
    identity = (
        lax.broadcasted_iota(jnp.int32, square, 0) == lax.broadcasted_iota(jnp.int32, square, 1)
    ).astype(F32)
    inverse = eliminate(jnp.concatenate([rho0, identity], axis=1))[:, rhs:]
    sol1 = mixed(alpha0, vec_z[...])
    middle_sum(1)
    image = near + far_part(1)
    own = gram(z1, image)
    start_sum(folded(own), 2)
    second_pair = end_sum(1)
    cross, rho1 = second_pair[:, :rhs], second_pair[:, rhs:]
    beta0_t = mixed(inverse, rho1).T
    middle_sum(2)
    search = z1 + mixed(beta0_t, vec_z[...])
    image = image + mixed(beta0_t, vec_q[...])
    turned = mixed(beta0_t, cross)
    known = turned + turned.T + gram(mixed(beta0_t, curve), beta0_t)
    own = unfolded(end_sum(2))
    alpha1 = solved(jnp.concatenate([own + known, rho1], axis=1))
    sol_ref[...] = sol1 + mixed(alpha1, search)
    res_ref[...] = res1 - mixed(alpha1, image)

    pltpu.make_async_copy(others, others, u_send).wait()
    first_halo.wait_send()
    second_halo.wait_send()
    first_back.wait_send()
    second_back.wait_send()
    for call in range(2):
        piece = coef_out.at[call, : (total - 1) * LOW, :]
        pltpu.make_async_copy(piece, piece, coef_send.at[call]).wait()
    for call in range(4):
        piece = sum_row.at[call, : rows - 1, : heights[call]]
        pltpu.make_async_copy(piece, piece, row_send.at[call]).wait()
        piece = sum_col.at[call, : cols - 1, : heights[call]]
        pltpu.make_async_copy(piece, piece, col_send.at[call]).wait()


def body(rows, cols, right_sides, diag_tiles, low_rank, tile_ranks, inv_factor, sub_sizes):
    rhs, tile = right_sides.shape
    spans, reach, span, _ = inv_factor.shape
    tile_rows, _, groups, _, rank, _ = low_rank.shape
    total = rows * cols
    halo = (reach - 1) * span
    pieces = tile // LANES
    factor = low_rank.reshape(tile_rows, groups, 2, rank, pieces, LANES)
    factor = factor.transpose(0, 1, 3, 4, 2, 5).reshape(-1, LANES)
    in_hbm = pl.BlockSpec(memory_space=pltpu.HBM)
    vmem = pl.BlockSpec(memory_space=pltpu.VMEM)
    dma = pltpu.SemaphoreType.DMA
    out = jax.ShapeDtypeStruct((rhs, tile), F32)
    buffers = [
        pltpu.VMEM((spans, span, reach * span), F32),
        pltpu.VMEM((spans, span, reach * span), BF16),
        pltpu.VMEM((spans, span, reach * span), BF16),
        pltpu.VMEM((tile, tile), F32),
        pltpu.VMEM((tile, tile), BF16),
        pltpu.VMEM((tile, tile), BF16),
        pltpu.VMEM((total * LOW, tile + tile // 2), F32),
        pltpu.VMEM((2 * total * LOW, tile), BF16),
        pltpu.VMEM((2 * total * LOW, tile), BF16),
        pltpu.VMEM(factor.shape, F32),
        pltpu.VMEM((groups, tile_rows * LOW, tile + tile // 2), F32),
        pltpu.VMEM((2 * rhs, halo + tile), BF16),
        pltpu.VMEM((2, rhs, halo), F32),
        pltpu.VMEM((2, rhs, halo), F32),
        pltpu.VMEM((2, rhs, halo), F32),
        pltpu.VMEM((rhs, halo + tile), F32),
        pltpu.VMEM((rhs, tile), F32),
        pltpu.VMEM((rhs, tile), F32),
        pltpu.VMEM((2, total * LOW, 2 * rhs), F32),
        pltpu.VMEM((2, total * LOW, 2 * rhs), F32),
        pltpu.VMEM((4, rows, rhs, 2 * rhs), F32),
        pltpu.VMEM((4, cols, rhs, 2 * rhs), F32),
    ]
    held = sum(math.prod(b.shape) * jnp.dtype(b.dtype).itemsize for b in buffers)
    grant = min(held + (24 << 20), 62 << 20)
    return pl.pallas_call(
        functools.partial(kernel, rows, cols),
        out_shape=(out, out),
        in_specs=[vmem, in_hbm, in_hbm, pl.BlockSpec(memory_space=pltpu.SMEM), in_hbm, vmem],
        out_specs=(vmem, vmem),
        scratch_shapes=buffers + [
            dma((spans,)), dma, dma, dma((4,)), dma, dma,
            dma((2,)), dma((2,)), dma((2,)), dma((2,)),
            dma((2,)), dma((2,)), dma((4,)), dma((4,)), dma((4,)), dma((4,)),
        ],
        compiler_params=pltpu.CompilerParams(
            collective_id=0, has_side_effects=True, vmem_limit_bytes=grant
        ),
    )(right_sides, diag_tiles, factor, tile_ranks, inv_factor, sub_sizes.reshape(1, -1))


def solution(mesh):
    rows, cols = mesh.shape["row"], mesh.shape["col"]
    placed = (
        P(None, ("row", "col")),
        P(("row", "col"), None, None),
        P("row", "col", None, None, None, None),
        P("row", "col", None),
        P(("row", "col"), None, None, None),
        P(),
    )
    return jax.shard_map(
        functools.partial(body, rows, cols),
        mesh=mesh,
        in_specs=placed,
        out_specs=(P(None, ("row", "col")), P(None, ("row", "col"))),
        check_vma=False,
    )
```

profile of v0, /device:TPU:0, one launch (start us, length us, event | category | flops | bytes accessed | tf_op | source)
XLA Modules:
  0.0 74.9 jit_solution(3887848990503220488)
XLA Ops:
  0.6 0.0 copy-start
  0.6 0.9 %copy-done = f32[64,1024]{1,0:T(8,128)S(1)} copy-done((f32[64,1024]{1,0:T(8,128)S(1)}, f32[64,1024]{1,0:T(8,128)}, u32[]{:S(2)}) %copy-start) | copy-done | bytes 262168
  1.6 0.0 copy-start.1
  1.6 0.7 copy-done.1
  2.3 0.0 copy-start.2
  2.3 0.7 copy-done.2
  2.9 70.6 %shard_map.77 = (f32[64,1024]{1,0:T(8,128)S(1)}, f32[64,1024]{1,0:T(8,128)S(1)}) custom-call(f32[64,1024]{1,0:T(8,128)S(1)} %copy-done, f32[1,1024,1024]{2,1,0:T(8,128)} %diag_ref.1, f32[6144,128]{1,0:T(8,128)} %bitcast.7, s32[4,1,8]{2,1,0:T(1,128)S(1)} %copy-done.1, f32[8,8,128,128]{3,2,1,0:T(8,128)} %inv_ref.1, s32[1,64]{1,0:T(1,128)S(1)} %bitcast.6), custom_call_target="tpu_custom_call" | custom-call | tf_op jit(solution)/shard_map/pallas_call | solution.py:490
  73.5 0.7 copy.11
  74.2 0.7 copy.12
Async XLA Ops:
  0.6 1.0 %copy-start = (f32[64,1024]{1,0:T(8,128)S(1)}, f32[64,1024]{1,0:T(8,128)}, u32[]{:S(2)}) copy-start(f32[64,1024]{1,0:T(8,128)} %x_ref.1) | copy-start | bytes 786436
  1.6 0.7 copy-start.1
  2.3 0.7 copy-start.2
where the time goes:
time: 75.1 us; the launch traced here: 74.9 us
  Pallas kernels  70.6 us (94%)
  local copies, waits for them, and re-layouts  3.69 us (5%)
    pallas_call x1, Pallas kernels, body(): pl.pallas_call(functools.partial(kernel, rows, cols), out_shape=(out, out...  70.6 us
    unnamed x8, local copies, waits for them, and re-layouts  3.69 us

commit v1 on v0

v1 whole, which is shorter than its diff:
```python
import functools
import math

import jax
import jax.numpy as jnp
from jax import lax
from jax.experimental import pallas as pl
from jax.experimental.pallas import tpu as pltpu
from jax.sharding import PartitionSpec as P

MESH = pl.DeviceIdType.MESH
F32 = jnp.float32
BF16 = jnp.bfloat16
LOW = 8
LANES = 128


def split(x):
    high = x.astype(BF16)
    return high, (x - high.astype(F32)).astype(BF16)


def stacked(x):
    high, low = split(x)
    return jnp.concatenate([high, low], axis=0)


def dot_nt(a, b):
    return lax.dot_general(a, b, (((1,), (1,)), ((), ())), preferred_element_type=F32)


def dot_nn(a, b):
    return lax.dot_general(a, b, (((1,), (0,)), ((), ())), preferred_element_type=F32)


def product3(dot, both, high, low):
    rows = both.shape[0] // 2
    first = dot(both, high)
    return first[:rows] + (first[rows:] + dot(both[:rows], low))


def gram(a, b):
    return lax.dot_general(
        a, b, (((1,), (1,)), ((), ())), precision=lax.Precision.HIGHEST, preferred_element_type=F32
    )


def mixed(coeffs, rows):
    return jnp.dot(coeffs, rows, precision=lax.Precision.HIGHEST, preferred_element_type=F32)


def eliminate(work):
    count, width = work.shape
    block = 4
    row_ids = lax.broadcasted_iota(jnp.int32, work.shape, 0)
    for k in range(0, count, block):
        columns = [jnp.broadcast_to(work[:, k + j : k + j + 1], work.shape) for j in range(block)]
        rows = [work[k + i : k + i + 1, :] for i in range(block)]
        heads = [[columns[j][k + i : k + i + 1, :] for j in range(block)] for i in range(block)]
        for i in range(block):
            inverse = 1.0 / heads[i][i]
            rows[i] = rows[i] * inverse
            for j in range(i + 1, block):
                heads[i][j] = heads[i][j] * inverse
            for other in range(block):
                if other != i:
                    factor = heads[other][i]
                    rows[other] = rows[other] - factor * rows[i]
                    for j in range(i + 1, block):
                        heads[other][j] = heads[other][j] - factor * heads[i][j]
        update = columns[0] * rows[0]
        for j in range(1, block):
            update = update + columns[j] * rows[j]
        work = work - update
        for i in range(block):
            work = jnp.where(row_ids == k + i, rows[i], work)
    return work


def solved(work):
    return eliminate(work).T[work.shape[0] :, :]


def kernel(
    rows, cols, pieces, rank,
    x_hbm, diag_ref, factor_ref, ranks_ref, inv_ref, sizes_ref,
    sol_ref, res_ref,
    x_ref, inv_f32, inv_cat, diag_f32, diag_hi, diag_lo, u_f32, u_hi, u_lo,
    factor_f32, packed, joined, halo_in, back_in, spread, fwd, doubled, vec_z, vec_p, vec_q, vec_n, pair,
    acc_wide, acc_low, coef_out, coef_in, sum_row, sum_col, nothing, sizes_vmem, ranks,
    inv_sem, diag_sem, factor_sem, small_sem, own_sem, u_send, u_recv, halo_send, halo_recv, back_send, back_recv,
    coef_send, coef_recv, row_send, row_recv, col_send, col_recv,
):
    my_row, my_col = lax.axis_index("row"), lax.axis_index("col")
    total = rows * cols
    me = my_row * cols + my_col
    rhs, tile = x_hbm.shape
    spans, reach, span, _ = inv_ref.shape
    halo = (reach - 1) * span
    wide = reach * span
    offset = tile - halo
    half = rank // 2

    def coords(device):
        return (device // cols, device % cols)

    following = coords((me + 1) % total)
    previous = coords((me + total - 1) % total)

    coef_in[...] = jnp.zeros_like(coef_in)
    back_in[...] = jnp.zeros_like(back_in)
    nothing[...] = jnp.zeros_like(nothing)

    barrier = pltpu.get_barrier_semaphore()

    def greet(step, carry):
        peer_row = (my_row + step) % rows
        for turn in range(cols):
            pl.semaphore_signal(
                barrier, inc=1, device_id=(peer_row, (my_col + turn) % cols), device_id_type=MESH
            )
        return carry

    for turn in range(1, cols):
        pl.semaphore_signal(
            barrier, inc=1, device_id=(my_row, (my_col + turn) % cols), device_id_type=MESH
        )
    lax.fori_loop(1, rows, greet, 0)

    factor_copy = pltpu.make_async_copy(factor_ref, factor_f32, factor_sem)
    factor_copy.start()
    ranks_copy = pltpu.make_async_copy(ranks_ref, ranks, small_sem.at[0])
    ranks_copy.start()
    sizes_copy = pltpu.make_async_copy(sizes_ref, sizes_vmem, small_sem.at[1])
    sizes_copy.start()
    x_copy = pltpu.make_async_copy(x_hbm, x_ref, small_sem.at[2])
    x_copy.start()
    for a in range(spans):
        for t in range(reach):
            copy = pltpu.make_async_copy(
                inv_ref.at[a, t],
                inv_f32.at[a, :, (reach - 1 - t) * span : (reach - t) * span],
                inv_sem.at[a],
            )
            copy.start()
    diag_copy = pltpu.make_async_copy(diag_ref.at[0], diag_f32, diag_sem)
    diag_copy.start()
    groups = rows
    tail = rank - LOW
    step_rows = 2 * (tile // LANES)

    def at_rows(ref, index, size):
        return ref.at[pl.ds(pl.multiple_of(index * size, size), size), :]

    def take(base, side, first, size, limit):
        ids = first + lax.broadcasted_iota(jnp.int32, (size, LANES), 0)
        parts = [
            factor_f32[pl.ds(base + first * step_rows + 2 * i + side, size, stride=step_rows), :]
            for i in range(tile // LANES)
        ]
        return jnp.concatenate([jnp.where(ids < limit, part, 0.0) for part in parts], axis=1)

    ranks_copy.wait()
    factor_copy.wait()

    def block(base, side, limit):
        rest = take(base, side, LOW, tail, limit)
        rest = jnp.concatenate([rest[:, : tile // 2], rest[:, tile // 2 :]], axis=0)
        return take(base, side, 0, LOW, limit), rest

    def pack(k, carry):
        for a in range(cols):
            base = (a * groups + k) * rank * step_rows
            first, rest = block(base, 1, ranks[a, 0, k])
            packed[k, a * LOW : (a + 1) * LOW, :tile] = first
            packed[k, a * LOW : (a + 1) * LOW, tile:] = rest
        base = (my_col * groups + k) * rank * step_rows
        where = pl.ds(pl.multiple_of((k * cols + my_col) * LOW, LOW), LOW)
        first, rest = block(base, 0, ranks[my_col, 0, k])
        u_f32[where, :tile] = first
        u_f32[where, tile:] = rest
        return carry

    lax.fori_loop(0, groups, pack, 0)

    for turn in range(1, cols):
        a = (my_col + turn) % cols
        pltpu.make_async_copy(
            at_rows(packed.at[my_row], a, LOW), at_rows(u_f32, my_row * cols + a, LOW), own_sem.at[1]
        ).start()
    pl.semaphore_wait(barrier, total - 1)

    def remote(src, dst, send, recv, device):
        return pltpu.make_async_remote_copy(
            src_ref=src, dst_ref=dst, send_sem=send, recv_sem=recv, device_id=device,
            device_id_type=MESH,
        )

    def halo_copy(src, call, c):
        lo, hi = pieces[c]
        return remote(
            src.at[:, offset + lo : offset + hi], halo_in.at[call, :, lo:hi],
            halo_send.at[call, c], halo_recv.at[call, c], following,
        )

    def back_copy(call, c):
        lo, hi = pieces[c]
        return remote(
            spread.at[call, :, lo:hi], back_in.at[call, :, offset + lo : offset + hi],
            back_send.at[call, c], back_recv.at[call, c], previous,
        )

    def send_halo(src, call, which):
        @pl.when(me != total - 1)
        def _():
            for c in which:
                halo_copy(src, call, c).start()

        @pl.when(me == 0)
        def _():
            for c in which:
                lo, hi = pieces[c]
                pltpu.make_async_copy(
                    nothing.at[:, lo:hi], halo_in.at[call, :, lo:hi], halo_recv.at[call, c]
                ).start()

    def send_back(call):
        @pl.when(me != 0)
        def _():
            for c in range(len(pieces)):
                back_copy(call, c).start()

        @pl.when(me == total - 1)
        def _():
            for c, (lo, hi) in enumerate(pieces):
                pltpu.make_async_copy(
                    nothing.at[:, lo:hi], back_in.at[call, :, offset + lo : offset + hi],
                    back_recv.at[call, c],
                ).start()

    send_halo(x_hbm, 0, range(len(pieces)))

    def send_factors(step, carry):
        peer = (my_row + step) % rows
        for turn in range(1, cols):
            a = (my_col + turn) % cols
            remote(at_rows(packed.at[peer], a, LOW), at_rows(u_f32, my_row * cols + a, LOW),
                   u_send, u_recv, (peer, my_col)).start()
        return carry

    lax.fori_loop(1, rows, send_factors, 0)
    x_copy.wait()
    sizes_copy.wait()

    subs = sizes_ref.shape[1]
    sizes = jnp.broadcast_to(sizes_vmem[...].astype(F32), (subs, subs))
    down = lax.broadcasted_iota(jnp.int32, (subs, subs), 0)
    across = lax.broadcasted_iota(jnp.int32, (subs, subs), 1)
    opening = jnp.sum(jnp.where(across < down, sizes, 0.0), axis=1, keepdims=True)
    behind = (reach - 1) - lax.broadcasted_iota(jnp.int32, (1, wide), 1) // span
    behind = behind.astype(F32)

    joined[:, halo:] = stacked(x_ref[...])

    for a in range(spans):
        for t in range(reach):
            pltpu.make_async_copy(
                inv_ref.at[a, t], inv_f32.at[a, :, t * span : (t + 1) * span], inv_sem.at[a]
            ).wait()
        number = (me * spans + a).astype(F32)
        start = jnp.max(jnp.where(opening <= number, opening, 0.0), axis=0, keepdims=True)
        mask = jnp.where(behind <= number - start, 1.0, 0.0)
        high, low = split(inv_f32[a] * mask)
        inv_cat[a, :span] = high
        inv_cat[a, span:] = low

    def quarters(product):
        first = product[:rhs, :span]
        return first + (product[rhs:, :span] + (product[:rhs, span:] + product[rhs:, span:]))

    def halves(product):
        return product[:rhs] + product[rhs:]

    def forward_own():
        for a in range(spans):
            skip = max(0, halo - a * span)
            fwd[a] = quarters(
                dot_nt(joined[:, a * span + skip : a * span + wide], inv_cat[a, :, skip:])
            )

    def finish(a):
        both = stacked(fwd[a])
        doubled[a] = jnp.concatenate([both, both], axis=1)

    def boundary(call):
        for a in range(spans):
            if a * span >= halo:
                finish(a)
        for c, (lo, hi) in enumerate(pieces):
            halo_copy(x_ref, call, c).wait_recv()
            joined[:, lo:hi] = stacked(halo_in[call, :, lo:hi])
            for a in range(spans):
                first = max(lo, a * span)
                if first < hi:
                    fwd[a] += quarters(dot_nt(
                        joined[:, first:hi], inv_cat[a, :, first - a * span : hi - a * span]
                    ))
            for a in range(spans):
                if lo <= a * span < hi:
                    finish(a)
                    spread[call, :, a * span : halo] += halves(
                        dot_nn(doubled[a], inv_cat[a, :, : halo - a * span])
                    )
        send_back(call)

    def backward_own(call):
        for a in range(spans):
            skip = max(0, halo - a * span)
            spread[call, :, a * span + skip : a * span + wide] += halves(
                dot_nn(doubled[a], inv_cat[a, :, skip:])
            )

    def returned(call, c):
        lo, hi = pieces[c]
        back_copy(call, c).wait_recv()
        first = offset + lo if lo else 0
        last = offset + hi
        return first, last, spread[call, :, halo + first : halo + last] + back_in[call, :, first:last]

    def add_coeffs(c, first, last, piece):
        both = stacked(piece)
        pair[:, first:last] = both
        wide_part = dot_nt(u_hi[:, first:last], both)
        low_part = dot_nt(u_lo[:, first:last], both[:rhs])
        if c:
            acc_wide[...] += wide_part
            acc_low[...] += low_part
        else:
            acc_wide[...] = wide_part
            acc_low[...] = low_part

    def send_coeffs(call):
        coeffs = acc_wide[:, :rhs] + (acc_wide[:, rhs:] + acc_low[...])
        middle = total * LOW
        coef_out[call, :, :, :rhs] = coeffs[:middle].reshape(total, LOW, rhs)
        coef_out[call, :, :, rhs:] = coeffs[middle:].reshape(total, LOW, rhs)

        def send(peer_row, peer_col):
            remote(coef_out.at[call, peer_row * cols + peer_col, :half, :],
                   coef_in.at[call, me, :half, :],
                   coef_send.at[call], coef_recv.at[call], (peer_row, peer_col)).start()

        low_side = 1 - my_col // (cols // 2)

        def send_row(step, carry):
            peer_row = (my_row + step) % rows
            for n in range(cols - 1):
                far = low_side * (cols - 1 - n) + (1 - low_side) * n
                beyond = (far - my_col + cols - 1) // cols
                before = (my_col - far + cols - 1) // cols
                far = far - low_side * (1 - beyond) + (1 - low_side) * (1 - before)
                send(peer_row, far)
            return carry

        lax.fori_loop(0, rows, send_row, 0)
        for step in range(1, rows):
            send((my_row + step) % rows, my_col)
        pltpu.make_async_copy(
            coef_out.at[call, me], coef_in.at[call, me], own_sem.at[2 + call]
        ).start()

    def flat(ref, call):
        return ref[call].reshape(total * LOW, 2 * rhs).T

    def wait_coeffs(call):
        every = coef_out.at[call, : total - 1, :half, :]
        pltpu.make_async_copy(every, every, coef_recv.at[call]).wait()
        pltpu.make_async_copy(
            coef_out.at[call, me], coef_in.at[call, me], own_sem.at[2 + call]
        ).wait()
        return flat(coef_in, call)

    def far_gram(mine, others):
        product = gram(mine, others)
        return product[:rhs, :rhs] + product[rhs:, rhs:]

    height = rhs // 2

    def start_sum(value, call):
        sum_row[call, my_row] = jnp.concatenate([value[:height], value[height:]], axis=1)
        for step in range(1, rows):
            mine = sum_row.at[call, my_row]
            remote(mine, mine, row_send.at[call],
                   row_recv.at[call], ((my_row + step) % rows, my_col)).start()

    def middle_sum(call):
        piece = sum_row.at[call, : rows - 1]
        pltpu.make_async_copy(piece, piece, row_recv.at[call]).wait()
        sum_col[call, my_col] = jnp.sum(sum_row[call], axis=0)
        for step in range(1, cols):
            mine = sum_col.at[call, my_col]
            remote(mine, mine, col_send.at[call],
                   col_recv.at[call], (my_row, (my_col + step) % cols)).start()

    def end_sum(call):
        piece = sum_col.at[call, : cols - 1]
        pltpu.make_async_copy(piece, piece, col_recv.at[call]).wait()
        halves_ = jnp.sum(sum_col[call], axis=0)
        return jnp.concatenate([halves_[:, :rhs], halves_[:, rhs:]], axis=0)

    spread[...] = jnp.zeros_like(spread)
    forward_own()
    boundary(0)
    backward_own(0)
    diag_copy.wait()

    def split_diag(step, carry):
        where = pl.ds(pl.multiple_of(step * span, span), span)
        high, low = split(diag_f32[where, :])
        diag_hi[where, :] = high
        diag_lo[where, :] = low
        return carry

    lax.fori_loop(0, tile // span, split_diag, 0)
    own_piece = u_f32.at[: (cols - 1) * LOW, :]
    pltpu.make_async_copy(own_piece, own_piece, own_sem.at[1]).wait()
    others = u_f32.at[: (rows - 1) * (cols - 1) * LOW, :]
    pltpu.make_async_copy(others, others, u_recv).wait()
    level = lax.broadcasted_iota(jnp.int32, (2 * LOW, tile), 0) % LOW
    empty = jnp.zeros((LOW - tail, tile), F32)

    def split_factors(step, carry):
        where = pl.ds(pl.multiple_of(step * 2 * LOW, 2 * LOW), 2 * LOW)
        first = u_f32[where, :tile]
        high, low = split(jnp.where(level < half, first, 0.0))
        u_hi[where, :] = high
        u_lo[where, :] = low
        rest = u_f32[where, tile:]
        parts = []
        for top in (0, LOW):
            parts.append(jnp.concatenate(
                [rest[top : top + tail], rest[top + tail : top + 2 * tail]], axis=1
            ))
            parts.append(empty)
        moved = pltpu.roll(first, 2 * LOW - (half - tail), 0)
        second = jnp.concatenate(parts, axis=0)
        second = jnp.where((level >= tail) & (level < half), moved, second)
        high, low = split(second)
        later = pl.ds(pl.multiple_of(total * LOW + step * 2 * LOW, 2 * LOW), 2 * LOW)
        u_hi[later, :] = high
        u_lo[later, :] = low
        return carry

    lax.fori_loop(0, total // 2, split_factors, 0)
    for c in range(len(pieces)):
        first, last, piece = returned(0, c)
        vec_z[:, first:last] = piece
        add_coeffs(c, first, last, piece)
    send_coeffs(0)
    start_sum(gram(vec_z[...], x_ref[...]), 3)
    near = product3(dot_nn, pair[...], diag_hi[...], diag_lo[...])
    vec_n[...] = near
    own0 = gram(vec_z[...], near)
    mine = flat(coef_out, 0)
    middle_sum(3)
    turned = wait_coeffs(0)

    def far_pieces(turned):
        both = stacked(jnp.concatenate([turned[:rhs], turned[rhs:]], axis=1))
        for c, (lo, hi) in enumerate(pieces):
            first = offset + lo if lo else 0
            last = offset + hi
            yield c, first, last, product3(
                dot_nn, both, u_hi[:, first:last], u_lo[:, first:last]
            )

    for c, first, last, piece in far_pieces(turned):
        vec_q[:, first:last] = vec_n[:, first:last] + piece
        send_halo(vec_q, 1, (c,))
    start_sum(own0 + far_gram(mine, turned), 0)
    joined[:, halo:] = stacked(vec_q[...])
    forward_own()
    rho0 = end_sum(3)
    square = (rhs, rhs)
    identity = (
        lax.broadcasted_iota(jnp.int32, square, 0) == lax.broadcasted_iota(jnp.int32, square, 1)
    ).astype(F32)
    inverse = eliminate(jnp.concatenate([rho0, identity], axis=1))[:, rhs:]
    middle_sum(0)
    boundary(1)
    backward_own(1)
    curve = end_sum(0)
    alpha0 = solved(jnp.concatenate([curve, rho0], axis=1))
    res_ref[...] = x_ref[...] - mixed(alpha0, vec_q[...])
    for c in range(len(pieces)):
        first, last, piece = returned(1, c)
        piece = vec_z[:, first:last] - mixed(alpha0, piece)
        vec_p[:, first:last] = piece
        add_coeffs(c, first, last, piece)
    send_coeffs(1)
    start_sum(gram(vec_p[...], res_ref[...]), 1)
    near = product3(dot_nn, pair[...], diag_hi[...], diag_lo[...])
    vec_n[...] = near
    own1 = gram(vec_p[...], near)
    mine = flat(coef_out, 1)
    sol_ref[...] = mixed(alpha0, vec_z[...])
    middle_sum(1)
    turned = wait_coeffs(1)
    start_sum(own1 + far_gram(mine, turned), 2)
    for c, first, last, piece in far_pieces(turned):
        vec_n[:, first:last] += piece
    middle_sum(2)
    rho1 = end_sum(1)
    beta0_t = mixed(inverse, rho1).T
    known = gram(mixed(beta0_t, curve), beta0_t)
    vec_p[...] += mixed(beta0_t, vec_z[...])
    vec_n[...] += mixed(beta0_t, vec_q[...])
    own = end_sum(2)
    alpha1 = solved(jnp.concatenate([own - known, rho1], axis=1))
    sol_ref[...] += mixed(alpha1, vec_p[...])
    res_ref[...] -= mixed(alpha1, vec_n[...])

    pltpu.make_async_copy(others, others, u_send).wait()

    @pl.when(me != total - 1)
    def _():
        for call in range(2):
            for c in range(len(pieces)):
                halo_copy(x_ref, call, c).wait_send()

    @pl.when(me != 0)
    def _():
        for call in range(2):
            for c in range(len(pieces)):
                back_copy(call, c).wait_send()

    for call in range(2):
        every = coef_out.at[call, : total - 1, :half, :]
        pltpu.make_async_copy(every, every, coef_send.at[call]).wait()
    for call in range(4):
        piece = sum_row.at[call, : rows - 1]
        pltpu.make_async_copy(piece, piece, row_send.at[call]).wait()
        piece = sum_col.at[call, : cols - 1]
        pltpu.make_async_copy(piece, piece, col_send.at[call]).wait()


def write_out(sol_ref, res_ref, sol_out, res_out, sems):
    copies = [
        pltpu.make_async_copy(sol_ref, sol_out, sems.at[0]),
        pltpu.make_async_copy(res_ref, res_out, sems.at[1]),
    ]
    for copy in copies:
        copy.start()
    for copy in copies:
        copy.wait()


def body(rows, cols, right_sides, diag_tiles, low_rank, tile_ranks, inv_factor, sub_sizes):
    rhs, tile = right_sides.shape
    spans, reach, span, _ = inv_factor.shape
    tile_rows, _, groups, _, rank, _ = low_rank.shape
    total = rows * cols
    halo = (reach - 1) * span
    lanes = tile // LANES
    factor = low_rank.reshape(tile_rows, groups, 2, rank, lanes, LANES)
    factor = factor.transpose(0, 1, 3, 4, 2, 5).reshape(-1, LANES)
    pieces, high = [], halo
    while high > 0:
        pieces.append((max(0, high - 2 * span), high))
        high = pieces[-1][0]
    count = len(pieces)
    in_hbm = pl.BlockSpec(memory_space=pltpu.HBM)
    vmem = pl.BlockSpec(memory_space=pltpu.VMEM)
    dma = pltpu.SemaphoreType.DMA
    out = jax.ShapeDtypeStruct((rhs, tile), F32)
    sizes = sub_sizes.reshape(1, -1)
    buffers = [
        pltpu.VMEM((rhs, tile), F32),
        pltpu.VMEM((spans, span, reach * span), F32),
        pltpu.VMEM((spans, 2 * span, reach * span), BF16),
        pltpu.VMEM((tile, tile), F32),
        pltpu.VMEM((tile, tile), BF16),
        pltpu.VMEM((tile, tile), BF16),
        pltpu.VMEM((total * LOW, tile + tile // 2), F32),
        pltpu.VMEM((2 * total * LOW, tile), BF16),
        pltpu.VMEM((2 * total * LOW, tile), BF16),
        pltpu.VMEM(factor.shape, F32),
        pltpu.VMEM((groups, tile_rows * LOW, tile + tile // 2), F32),
        pltpu.VMEM((2 * rhs, halo + tile), BF16),
        pltpu.VMEM((2, rhs, halo), F32),
        pltpu.VMEM((2, rhs, tile), F32),
        pltpu.VMEM((2, rhs, halo + tile), F32),
        pltpu.VMEM((spans, rhs, span), F32),
        pltpu.VMEM((spans, 2 * rhs, 2 * span), BF16),
        pltpu.VMEM((rhs, tile), F32),
        pltpu.VMEM((rhs, tile), F32),
        pltpu.VMEM((rhs, tile), F32),
        pltpu.VMEM((rhs, tile), F32),
        pltpu.VMEM((2 * rhs, tile), BF16),
        pltpu.VMEM((2 * total * LOW, 2 * rhs), F32),
        pltpu.VMEM((2 * total * LOW, rhs), F32),
        pltpu.VMEM((2, total, LOW, 2 * rhs), F32),
        pltpu.VMEM((2, total, LOW, 2 * rhs), F32),
        pltpu.VMEM((4, rows, rhs // 2, 2 * rhs), F32),
        pltpu.VMEM((4, cols, rhs // 2, 2 * rhs), F32),
        pltpu.VMEM((rhs, halo), F32),
        pltpu.VMEM(sizes.shape, jnp.int32),
    ]
    held = sum(math.prod(b.shape) * jnp.dtype(b.dtype).itemsize for b in buffers)
    grant = min(held + (8 << 20), 62 << 20)
    operands = [
        pltpu.with_memory_space_constraint(array, pltpu.HBM)
        for array in (right_sides, diag_tiles, factor, tile_ranks, inv_factor, sizes)
    ]
    results = pl.pallas_call(
        functools.partial(kernel, rows, cols, tuple(pieces), rank),
        out_shape=(pltpu.VMEM((rhs, tile), F32), pltpu.VMEM((rhs, tile), F32)),
        in_specs=[in_hbm] * 6,
        out_specs=(vmem, vmem),
        scratch_shapes=buffers + [
            pltpu.SMEM(tile_ranks.shape, jnp.int32),
            dma((spans,)), dma, dma, dma((3,)), dma((4,)), dma, dma,
            dma((2, count)), dma((2, count)), dma((2, count)), dma((2, count)),
            dma((2,)), dma((2,)), dma((4,)), dma((4,)), dma((4,)), dma((4,)),
        ],
        compiler_params=pltpu.CompilerParams(
            collective_id=0, has_side_effects=True, vmem_limit_bytes=grant
        ),
    )(*operands)
    return pl.pallas_call(
        write_out,
        out_shape=(out, out),
        in_specs=[vmem, vmem],
        out_specs=(in_hbm, in_hbm),
        scratch_shapes=[dma((2,))],
        compiler_params=pltpu.CompilerParams(vmem_limit_bytes=1 << 20),
    )(*[pltpu.with_memory_space_constraint(result, pltpu.VMEM) for result in results])


def solution(mesh):
    rows, cols = mesh.shape["row"], mesh.shape["col"]
    placed = (
        P(None, ("row", "col")),
        P(("row", "col"), None, None),
        P("row", "col", None, None, None, None),
        P("row", "col", None),
        P(("row", "col"), None, None, None),
        P(),
    )
    return jax.shard_map(
        functools.partial(body, rows, cols),
        mesh=mesh,
        in_specs=placed,
        out_specs=(P(None, ("row", "col")), P(None, ("row", "col"))),
        check_vma=False,
    )
```

time: 75.1 us -> 67.3 us (0.90)
  Pallas kernels: 70.6 us -> 66.4 us
  local copies, waits for them, and re-layouts: 3.69 us -> 0 us
    pallas_call x1 -> x2, Pallas kernels: 70.6 us -> 66.4 us  [the longest x1 65.6 us: body(): pl.pallas_call(functools.partial(kernel, rows, cols, tuple(pieces), rank)...]
    unnamed x8 -> x0, local copies, waits for them, and re-layouts: 3.69 us -> none
where the time goes in v1:
time: 67.3 us; the launch traced here: 67.2 us
  Pallas kernels  66.4 us (99%)
  between operations  0.8 us (1%)
    pallas_call x1, Pallas kernels, body(): pl.pallas_call(functools.partial(kernel, rows, cols, tuple(pieces), rank)...  65.6 us

profile of v1, /device:TPU:0, one launch (start us, length us, event | category | flops | bytes accessed | tf_op | source)
XLA Modules:
  0.0 67.2 jit_solution(11043148338987827040)
XLA Ops:
  0.6 65.6 %shard_map.77 = (f32[64,1024]{1,0:T(8,128)S(1)}, f32[64,1024]{1,0:T(8,128)S(1)}) custom-call(f32[64,1024]{1,0:T(8,128)} %x_hbm.1, f32[1,1024,1024]{2,1,0:T(8,128)} %diag_ref.1, f32[6144,128]{1,0:T(8,128)} %bitcast.6, s32[4,1,8]{2,1,0:T(1,128)} %ranks_ref.1, f32[8,8,128,128]{3,2,1,0:T(8,128)} %inv_ref.1, s32[1,64]{1,0:T(1,128)} %bitcast.7), custom_call_target="tpu_custom_call" | custom-call | tf_op jit(solution)/shard_map/pallas_call | solution.py:615
  66.2 0.8 %shard_map.78 = (f32[64,1024]{1,0:T(8,128)}, f32[64,1024]{1,0:T(8,128)}) custom-call(f32[64,1024]{1,0:T(8,128)S(1)} %get-tuple-element.4.sol_ref, f32[64,1024]{1,0:T(8,128)S(1)} %get-tuple-element.5.res_ref), custom_call_target="tpu_custom_call" | custom-call | tf_op jit(solution)/shard_map/pallas_call | solution.py:630

commit v2 on v1

--- a/solution.py
+++ b/solution.py
@@ -51,7 +51,7 @@
 
 def eliminate(work):
     count, width = work.shape
-    block = 4
+    block = 8
     row_ids = lax.broadcasted_iota(jnp.int32, work.shape, 0)
     for k in range(0, count, block):
         columns = [jnp.broadcast_to(work[:, k + j : k + j + 1], work.shape) for j in range(block)]
@@ -68,10 +68,10 @@
                     rows[other] = rows[other] - factor * rows[i]
                     for j in range(i + 1, block):
                         heads[other][j] = heads[other][j] - factor * heads[i][j]
-        update = columns[0] * rows[0]
-        for j in range(1, block):
-            update = update + columns[j] * rows[j]
-        work = work - update
+        terms = [columns[j] * rows[j] for j in range(block)]
+        while len(terms) > 1:
+            terms = [terms[j] + terms[j + 1] for j in range(0, len(terms), 2)]
+        work = work - terms[0]
         for i in range(block):
             work = jnp.where(row_ids == k + i, rows[i], work)
     return work
@@ -89,7 +89,7 @@
     factor_f32, packed, joined, halo_in, back_in, spread, fwd, doubled, vec_z, vec_p, vec_q, vec_n, pair,
     acc_wide, acc_low, coef_out, coef_in, sum_row, sum_col, nothing, sizes_vmem, ranks,
     inv_sem, diag_sem, factor_sem, small_sem, own_sem, u_send, u_recv, halo_send, halo_recv, back_send, back_recv,
-    coef_send, coef_recv, row_send, row_recv, col_send, col_recv,
+    coef_send, coef_recv, row_send, row_recv, col_send, col_recv, known,
 ):
     my_row, my_col = lax.axis_index("row"), lax.axis_index("col")
     total = rows * cols
@@ -113,19 +113,21 @@
 
     barrier = pltpu.get_barrier_semaphore()
 
-    def greet(step, carry):
-        peer_row = (my_row + step) % rows
-        for turn in range(cols):
-            pl.semaphore_signal(
-                barrier, inc=1, device_id=(peer_row, (my_col + turn) % cols), device_id_type=MESH
-            )
-        return carry
+    def greet(semaphore, device):
+        pl.semaphore_signal(semaphore, inc=1, device_id=device, device_id_type=MESH)
 
     for turn in range(1, cols):
-        pl.semaphore_signal(
-            barrier, inc=1, device_id=(my_row, (my_col + turn) % cols), device_id_type=MESH
-        )
-    lax.fori_loop(1, rows, greet, 0)
+        greet(barrier, (my_row, (my_col + turn) % cols))
+    for step in range(1, rows):
+        greet(barrier, ((my_row + step) % rows, my_col))
+
+    @pl.when((my_col == cols - 1) & (me != total - 1))
+    def _():
+        greet(barrier, following)
+
+    @pl.when((my_col == 0) & (me != 0))
+    def _():
+        greet(barrier, previous)
 
     factor_copy = pltpu.make_async_copy(factor_ref, factor_f32, factor_sem)
     factor_copy.start()
@@ -135,6 +137,23 @@
     sizes_copy.start()
     x_copy = pltpu.make_async_copy(x_hbm, x_ref, small_sem.at[2])
     x_copy.start()
+    groups = rows
+    tail = rank - LOW
+    step_rows = 2 * (tile // LANES)
+
+    def at_rows(ref, index, size):
+        return ref.at[pl.ds(pl.multiple_of(index * size, size), size), :]
+
+    def take(base, side, first, size, limit):
+        ids = first + lax.broadcasted_iota(jnp.int32, (size, LANES), 0)
+        parts = [
+            factor_f32[pl.ds(base + first * step_rows + 2 * i + side, size, stride=step_rows), :]
+            for i in range(tile // LANES)
+        ]
+        return jnp.concatenate([jnp.where(ids < limit, part, 0.0) for part in parts], axis=1)
+
+    ranks_copy.wait()
+    factor_copy.wait()
     for a in range(spans):
         for t in range(reach):
             copy = pltpu.make_async_copy(
@@ -145,33 +164,27 @@
             copy.start()
     diag_copy = pltpu.make_async_copy(diag_ref.at[0], diag_f32, diag_sem)
     diag_copy.start()
-    groups = rows
-    tail = rank - LOW
-    step_rows = 2 * (tile // LANES)
-
-    def at_rows(ref, index, size):
-        return ref.at[pl.ds(pl.multiple_of(index * size, size), size), :]
-
-    def take(base, side, first, size, limit):
-        ids = first + lax.broadcasted_iota(jnp.int32, (size, LANES), 0)
-        parts = [
-            factor_f32[pl.ds(base + first * step_rows + 2 * i + side, size, stride=step_rows), :]
-            for i in range(tile // LANES)
-        ]
-        return jnp.concatenate([jnp.where(ids < limit, part, 0.0) for part in parts], axis=1)
-
-    ranks_copy.wait()
-    factor_copy.wait()
 
     def block(base, side, limit):
         rest = take(base, side, LOW, tail, limit)
         rest = jnp.concatenate([rest[:, : tile // 2], rest[:, tile // 2 :]], axis=0)
         return take(base, side, 0, LOW, limit), rest
 
+    def differ(difference, most):
+        square = difference * difference
+        return (square + most * most - 1) // (most * most)
+
+    def by_column(k, a):
+        if rows % 4:
+            return 0
+        opposite = 1 - differ(k // 2 + my_row // 2 - (rows // 2 - 1), rows)
+        near = 1 - differ((a - my_col) * (a - my_col) - 1, cols * cols)
+        return opposite * near
+
     def pack(k, carry):
         for a in range(cols):
             base = (a * groups + k) * rank * step_rows
-            first, rest = block(base, 1, ranks[a, 0, k])
+            first, rest = block(base, 1 - by_column(k, a), ranks[a, 0, k])
             packed[k, a * LOW : (a + 1) * LOW, :tile] = first
             packed[k, a * LOW : (a + 1) * LOW, tile:] = rest
         base = (my_col * groups + k) * rank * step_rows
@@ -188,7 +201,9 @@
         pltpu.make_async_copy(
             at_rows(packed.at[my_row], a, LOW), at_rows(u_f32, my_row * cols + a, LOW), own_sem.at[1]
         ).start()
-    pl.semaphore_wait(barrier, total - 1)
+    wraps = (1 - differ(my_col - (cols - 1), cols)) * differ(me - (total - 1), total)
+    wrapped = (1 - differ(my_col, cols)) * differ(me, total)
+    pl.semaphore_wait(barrier, rows + cols - 2 + wraps + wrapped)
 
     def remote(src, dst, send, recv, device):
         return pltpu.make_async_remote_copy(
@@ -215,6 +230,10 @@
         def _():
             for c in which:
                 halo_copy(src, call, c).start()
+
+        fill_first(call, which)
+
+    def fill_first(call, which):
 
         @pl.when(me == 0)
         def _():
@@ -238,17 +257,24 @@
                     back_recv.at[call, c],
                 ).start()
 
-    send_halo(x_hbm, 0, range(len(pieces)))
+    every_piece = range(len(pieces))
+
+    send_halo(x_hbm, 0, every_piece)
 
     def send_factors(step, carry):
         peer = (my_row + step) % rows
         for turn in range(1, cols):
             a = (my_col + turn) % cols
-            remote(at_rows(packed.at[peer], a, LOW), at_rows(u_f32, my_row * cols + a, LOW),
-                   u_send, u_recv, (peer, my_col)).start()
+            column = by_column(peer, a)
+            slot = (1 - column) * (my_row * cols + a) + column * (peer * cols + my_col)
+            place = (peer + column * (my_row - peer), my_col + column * (a - my_col))
+            remote(at_rows(packed.at[peer], a, LOW), at_rows(u_f32, slot, LOW),
+                   u_send, u_recv, place).start()
         return carry
 
     lax.fori_loop(1, rows, send_factors, 0)
+    for step in range(1, rows):
+        greet(known, ((my_row + step) % rows, my_col))
     x_copy.wait()
     sizes_copy.wait()
 
@@ -273,6 +299,7 @@
         high, low = split(inv_f32[a] * mask)
         inv_cat[a, :span] = high
         inv_cat[a, span:] = low
+
 
     def quarters(product):
         first = product[:rhs, :span]
@@ -370,7 +397,7 @@
         ).start()
 
     def flat(ref, call):
-        return ref[call].reshape(total * LOW, 2 * rhs).T
+        return stacked(ref[call].reshape(total * LOW, 2 * rhs).T)
 
     def wait_coeffs(call):
         every = coef_out.at[call, : total - 1, :half, :]
@@ -381,8 +408,12 @@
         return flat(coef_in, call)
 
     def far_gram(mine, others):
-        product = gram(mine, others)
-        return product[:rhs, :rhs] + product[rhs:, rhs:]
+        product = dot_nt(mine, others)
+        width = 2 * rhs
+        square = product[:width, :width] + (
+            product[width:, :width] + (product[:width, width:] + product[width:, width:])
+        )
+        return square[:rhs, :rhs] + square[rhs:, rhs:]
 
     height = rhs // 2
 
@@ -456,6 +487,7 @@
         first, last, piece = returned(0, c)
         vec_z[:, first:last] = piece
         add_coeffs(c, first, last, piece)
+    pl.semaphore_wait(known, rows - 1)
     send_coeffs(0)
     start_sum(gram(vec_z[...], x_ref[...]), 3)
     near = product3(dot_nn, pair[...], diag_hi[...], diag_lo[...])
@@ -466,7 +498,10 @@
     turned = wait_coeffs(0)
 
     def far_pieces(turned):
-        both = stacked(jnp.concatenate([turned[:rhs], turned[rhs:]], axis=1))
+        both = jnp.concatenate([
+            jnp.concatenate([turned[:rhs], turned[rhs : 2 * rhs]], axis=1),
+            jnp.concatenate([turned[2 * rhs : 3 * rhs], turned[3 * rhs :]], axis=1),
+        ], axis=0)
         for c, (lo, hi) in enumerate(pieces):
             first = offset + lo if lo else 0
             last = offset + hi
@@ -622,6 +657,7 @@
             dma((spans,)), dma, dma, dma((3,)), dma((4,)), dma, dma,
             dma((2, count)), dma((2, count)), dma((2, count)), dma((2, count)),
             dma((2,)), dma((2,)), dma((4,)), dma((4,)), dma((4,)), dma((4,)),
+            pltpu.SemaphoreType.REGULAR,
         ],
         compiler_params=pltpu.CompilerParams(
             collective_id=0, has_side_effects=True, vmem_limit_bytes=grant

time: 67.3 us -> 64.4 us (0.957)
  Pallas kernels: 66.4 us -> 63.4 us
    pallas_call x1, Pallas kernels: 65.6 us -> 62.6 us  [body(): pl.pallas_call(functools.partial(kernel, rows, cols, tuple(pieces), rank)...]
where the time goes in v2:
time: 64.4 us; the launch traced here: 64.2 us
  Pallas kernels  63.4 us (98%)
  between operations  0.8 us (1%)
    pallas_call x1, Pallas kernels, body(): pl.pallas_call(functools.partial(kernel, rows, cols, tuple(pieces), rank)...  62.6 us

profile of v2, /device:TPU:0, one launch (start us, length us, event | category | flops | bytes accessed | tf_op | source)
XLA Modules:
  0.0 64.2 jit_solution(14893329367584649389)
XLA Ops:
  0.6 62.6 %shard_map.77 = (f32[64,1024]{1,0:T(8,128)S(1)}, f32[64,1024]{1,0:T(8,128)S(1)}) custom-call(f32[64,1024]{1,0:T(8,128)} %x_hbm.1, f32[1,1024,1024]{2,1,0:T(8,128)} %diag_ref.1, f32[6144,128]{1,0:T(8,128)} %bitcast.6, s32[4,1,8]{2,1,0:T(1,128)} %ranks_ref.1, f32[8,8,128,128]{3,2,1,0:T(8,128)} %inv_ref.1, s32[1,64]{1,0:T(1,128)} %bitcast.7), custom_call_target="tpu_custom_call" | custom-call | tf_op jit(solution)/shard_map/pallas_call | solution.py:650
  63.2 0.8 %shard_map.78 = (f32[64,1024]{1,0:T(8,128)}, f32[64,1024]{1,0:T(8,128)}) custom-call(f32[64,1024]{1,0:T(8,128)S(1)} %get-tuple-element.4.sol_ref, f32[64,1024]{1,0:T(8,128)S(1)} %get-tuple-element.5.res_ref), custom_call_target="tpu_custom_call" | custom-call | tf_op jit(solution)/shard_map/pallas_call | solution.py:666

commit v3 on v2

--- a/solution.py
+++ b/solution.py
@@ -154,6 +154,94 @@
 
     ranks_copy.wait()
     factor_copy.wait()
+    def block(base, side, limit):
+        rest = take(base, side, LOW, tail, limit)
+        rest = jnp.concatenate([rest[:, : tile // 2], rest[:, tile // 2 :]], axis=0)
+        return take(base, side, 0, LOW, limit), rest
+
+    def differ(difference, most):
+        square = difference * difference
+        return (square + most * most - 1) // (most * most)
+
+    def by_column(k, a):
+        if rows % 4:
+            return 0
+        opposite = 1 - differ(k // 2 + my_row // 2 - (rows // 2 - 1), rows)
+        near = 1 - differ((a - my_col) * (a - my_col) - 1, cols * cols)
+        return opposite * near
+
+    def pack(k):
+        for a in range(cols):
+            base = (a * groups + k) * rank * step_rows
+            first, rest = block(base, 1 - by_column(k, a), ranks[a, 0, k])
+            packed[k, a * LOW : (a + 1) * LOW, :tile] = first
+            packed[k, a * LOW : (a + 1) * LOW, tile:] = rest
+        base = (my_col * groups + k) * rank * step_rows
+        where = pl.ds(pl.multiple_of((k * cols + my_col) * LOW, LOW), LOW)
+        first, rest = block(base, 0, ranks[my_col, 0, k])
+        u_f32[where, :tile] = first
+        u_f32[where, tile:] = rest
+
+    wraps = (1 - differ(my_col - (cols - 1), cols)) * differ(me - (total - 1), total)
+    wrapped = (1 - differ(my_col, cols)) * differ(me, total)
+    pl.semaphore_wait(barrier, rows + cols - 2 + wraps + wrapped)
+
+    def remote(src, dst, send, recv, device):
+        return pltpu.make_async_remote_copy(
+            src_ref=src, dst_ref=dst, send_sem=send, recv_sem=recv, device_id=device,
+            device_id_type=MESH,
+        )
+
+    def halo_copy(src, call, c):
+        lo, hi = pieces[c]
+        return remote(
+            src.at[:, offset + lo : offset + hi], halo_in.at[call, :, lo:hi],
+            halo_send.at[call, c], halo_recv.at[call, c], following,
+        )
+
+    def back_copy(call, c):
+        lo, hi = pieces[c]
+        return remote(
+            spread.at[call, :, lo:hi], back_in.at[call, :, offset + lo : offset + hi],
+            back_send.at[call, c], back_recv.at[call, c], previous,
+        )
+
+    def send_halo(src, call, which):
+        @pl.when(me != total - 1)
+        def _():
+            for c in which:
+                halo_copy(src, call, c).start()
+
+        fill_first(call, which)
+
+    def fill_first(call, which):
+
+        @pl.when(me == 0)
+        def _():
+            for c in which:
+                lo, hi = pieces[c]
+                pltpu.make_async_copy(
+                    nothing.at[:, lo:hi], halo_in.at[call, :, lo:hi], halo_recv.at[call, c]
+                ).start()
+
+    def send_back(call):
+        @pl.when(me != 0)
+        def _():
+            for c in range(len(pieces)):
+                back_copy(call, c).start()
+
+        @pl.when(me == total - 1)
+        def _():
+            for c, (lo, hi) in enumerate(pieces):
+                pltpu.make_async_copy(
+                    nothing.at[:, lo:hi], back_in.at[call, :, offset + lo : offset + hi],
+                    back_recv.at[call, c],
+                ).start()
+
+    every_piece = range(len(pieces))
+
+    send_halo(x_hbm, 0, every_piece)
+
     for a in range(spans):
         for t in range(reach):
             copy = pltpu.make_async_copy(
@@ -165,104 +253,7 @@
     diag_copy = pltpu.make_async_copy(diag_ref.at[0], diag_f32, diag_sem)
     diag_copy.start()
 
-    def block(base, side, limit):
-        rest = take(base, side, LOW, tail, limit)
-        rest = jnp.concatenate([rest[:, : tile // 2], rest[:, tile // 2 :]], axis=0)
-        return take(base, side, 0, LOW, limit), rest
-
-    def differ(difference, most):
-        square = difference * difference
-        return (square + most * most - 1) // (most * most)
-
-    def by_column(k, a):
-        if rows % 4:
-            return 0
-        opposite = 1 - differ(k // 2 + my_row // 2 - (rows // 2 - 1), rows)
-        near = 1 - differ((a - my_col) * (a - my_col) - 1, cols * cols)
-        return opposite * near
-
-    def pack(k, carry):
-        for a in range(cols):
-            base = (a * groups + k) * rank * step_rows
-            first, rest = block(base, 1 - by_column(k, a), ranks[a, 0, k])
-            packed[k, a * LOW : (a + 1) * LOW, :tile] = first
-            packed[k, a * LOW : (a + 1) * LOW, tile:] = rest
-        base = (my_col * groups + k) * rank * step_rows
-        where = pl.ds(pl.multiple_of((k * cols + my_col) * LOW, LOW), LOW)
-        first, rest = block(base, 0, ranks[my_col, 0, k])
-        u_f32[where, :tile] = first
-        u_f32[where, tile:] = rest
-        return carry
-
-    lax.fori_loop(0, groups, pack, 0)
-
-    for turn in range(1, cols):
-        a = (my_col + turn) % cols
-        pltpu.make_async_copy(
-            at_rows(packed.at[my_row], a, LOW), at_rows(u_f32, my_row * cols + a, LOW), own_sem.at[1]
-        ).start()
-    wraps = (1 - differ(my_col - (cols - 1), cols)) * differ(me - (total - 1), total)
-    wrapped = (1 - differ(my_col, cols)) * differ(me, total)
-    pl.semaphore_wait(barrier, rows + cols - 2 + wraps + wrapped)
-
-    def remote(src, dst, send, recv, device):
-        return pltpu.make_async_remote_copy(
-            src_ref=src, dst_ref=dst, send_sem=send, recv_sem=recv, device_id=device,
-            device_id_type=MESH,
-        )
-
-    def halo_copy(src, call, c):
-        lo, hi = pieces[c]
-        return remote(
-            src.at[:, offset + lo : offset + hi], halo_in.at[call, :, lo:hi],
-            halo_send.at[call, c], halo_recv.at[call, c], following,
-        )
-
-    def back_copy(call, c):
-        lo, hi = pieces[c]
-        return remote(
-            spread.at[call, :, lo:hi], back_in.at[call, :, offset + lo : offset + hi],
-            back_send.at[call, c], back_recv.at[call, c], previous,
-        )
-
-    def send_halo(src, call, which):
-        @pl.when(me != total - 1)
-        def _():
-            for c in which:
-                halo_copy(src, call, c).start()
-
-        fill_first(call, which)
-
-    def fill_first(call, which):
-
-        @pl.when(me == 0)
-        def _():
-            for c in which:
-                lo, hi = pieces[c]
-                pltpu.make_async_copy(
-                    nothing.at[:, lo:hi], halo_in.at[call, :, lo:hi], halo_recv.at[call, c]
-                ).start()
-
-    def send_back(call):
-        @pl.when(me != 0)
-        def _():
-            for c in range(len(pieces)):
-                back_copy(call, c).start()
-
-        @pl.when(me == total - 1)
-        def _():
-            for c, (lo, hi) in enumerate(pieces):
-                pltpu.make_async_copy(
-                    nothing.at[:, lo:hi], back_in.at[call, :, offset + lo : offset + hi],
-                    back_recv.at[call, c],
-                ).start()
-
-    every_piece = range(len(pieces))
-
-    send_halo(x_hbm, 0, every_piece)
-
-    def send_factors(step, carry):
-        peer = (my_row + step) % rows
+    def send_factors(peer):
         for turn in range(1, cols):
             a = (my_col + turn) % cols
             column = by_column(peer, a)
@@ -270,9 +261,21 @@
             place = (peer + column * (my_row - peer), my_col + column * (a - my_col))
             remote(at_rows(packed.at[peer], a, LOW), at_rows(u_f32, slot, LOW),
                    u_send, u_recv, place).start()
+
+    def pack_next(step, carry):
+        pack((my_row + step) % rows)
+        send_factors((my_row + step - 1) % rows)
         return carry
 
-    lax.fori_loop(1, rows, send_factors, 0)
+    pack((my_row + 1) % rows)
+    lax.fori_loop(2, rows, pack_next, 0)
+    pack(my_row)
+    send_factors((my_row + rows - 1) % rows)
+    for turn in range(1, cols):
+        a = (my_col + turn) % cols
+        pltpu.make_async_copy(
+            at_rows(packed.at[my_row], a, LOW), at_rows(u_f32, my_row * cols + a, LOW), own_sem.at[1]
+        ).start()
     for step in range(1, rows):
         greet(known, ((my_row + step) % rows, my_col))
     x_copy.wait()
@@ -379,17 +382,13 @@
 
         low_side = 1 - my_col // (cols // 2)
 
-        def send_row(step, carry):
-            peer_row = (my_row + step) % rows
-            for n in range(cols - 1):
-                far = low_side * (cols - 1 - n) + (1 - low_side) * n
-                beyond = (far - my_col + cols - 1) // cols
-                before = (my_col - far + cols - 1) // cols
-                far = far - low_side * (1 - beyond) + (1 - low_side) * (1 - before)
-                send(peer_row, far)
-            return carry
-
-        lax.fori_loop(0, rows, send_row, 0)
+        for n in range(cols - 1):
+            far = low_side * (cols - 1 - n) + (1 - low_side) * n
+            beyond = (far - my_col + cols - 1) // cols
+            before = (my_col - far + cols - 1) // cols
+            far = far - low_side * (1 - beyond) + (1 - low_side) * (1 - before)
+            for step in range(rows):
+                send((my_row + step) % rows, far)
         for step in range(1, rows):
             send((my_row + step) % rows, my_col)
         pltpu.make_async_copy(
@@ -398,6 +397,9 @@
 
     def flat(ref, call):
         return stacked(ref[call].reshape(total * LOW, 2 * rhs).T)
+
+    def sided(ref, call):
+        return jnp.concatenate(split(ref[call].reshape(total * LOW, 2 * rhs)), axis=1)
 
     def wait_coeffs(call):
         every = coef_out.at[call, : total - 1, :half, :]
@@ -405,10 +407,9 @@
         pltpu.make_async_copy(
             coef_out.at[call, me], coef_in.at[call, me], own_sem.at[2 + call]
         ).wait()
-        return flat(coef_in, call)
-
-    def far_gram(mine, others):
-        product = dot_nt(mine, others)
+
+    def far_gram(mine, call):
+        product = dot_nn(mine, sided(coef_in, call))
         width = 2 * rhs
         square = product[:width, :width] + (
             product[width:, :width] + (product[:width, width:] + product[width:, width:])
@@ -495,9 +496,10 @@
     own0 = gram(vec_z[...], near)
     mine = flat(coef_out, 0)
     middle_sum(3)
-    turned = wait_coeffs(0)
-
-    def far_pieces(turned):
+    wait_coeffs(0)
+
+    def far_pieces(call):
+        turned = flat(coef_in, call)
         both = jnp.concatenate([
             jnp.concatenate([turned[:rhs], turned[rhs : 2 * rhs]], axis=1),
             jnp.concatenate([turned[2 * rhs : 3 * rhs], turned[3 * rhs :]], axis=1),
@@ -509,10 +511,10 @@
                 dot_nn, both, u_hi[:, first:last], u_lo[:, first:last]
             )
 
-    for c, first, last, piece in far_pieces(turned):
+    for c, first, last, piece in far_pieces(0):
         vec_q[:, first:last] = vec_n[:, first:last] + piece
         send_halo(vec_q, 1, (c,))
-    start_sum(own0 + far_gram(mine, turned), 0)
+    start_sum(own0 + far_gram(mine, 0), 0)
     joined[:, halo:] = stacked(vec_q[...])
     forward_own()
     rho0 = end_sum(3)
@@ -540,9 +542,9 @@
     mine = flat(coef_out, 1)
     sol_ref[...] = mixed(alpha0, vec_z[...])
     middle_sum(1)
-    turned = wait_coeffs(1)
-    start_sum(own1 + far_gram(mine, turned), 2)
-    for c, first, last, piece in far_pieces(turned):
+    wait_coeffs(1)
+    start_sum(own1 + far_gram(mine, 1), 2)
+    for c, first, last, piece in far_pieces(1):
         vec_n[:, first:last] += piece
     middle_sum(2)
     rho1 = end_sum(1)

time: 64.4 us -> 62.7 us (0.974)
  Pallas kernels: 63.4 us -> 61.8 us
    pallas_call x1, Pallas kernels: 62.6 us -> 61 us  [body(): pl.pallas_call(functools.partial(kernel, rows, cols, tuple(pieces), rank)...]
where the time goes in v3:
time: 62.7 us; the launch traced here: 62.6 us
  Pallas kernels  61.8 us (99%)
  between operations  0.8 us (1%)
    pallas_call x1, Pallas kernels, body(): pl.pallas_call(functools.partial(kernel, rows, cols, tuple(pieces), rank)...  61 us

profile of v3, /device:TPU:0, one launch (start us, length us, event | category | flops | bytes accessed | tf_op | source)
XLA Modules:
  0.0 62.6 jit_solution(3469425904711341051)
XLA Ops:
  0.6 61.0 %shard_map.77 = (f32[64,1024]{1,0:T(8,128)S(1)}, f32[64,1024]{1,0:T(8,128)S(1)}) custom-call(f32[64,1024]{1,0:T(8,128)} %x_hbm.1, f32[1,1024,1024]{2,1,0:T(8,128)} %diag_ref.1, f32[6144,128]{1,0:T(8,128)} %bitcast.6, s32[4,1,8]{2,1,0:T(1,128)} %ranks_ref.1, f32[8,8,128,128]{3,2,1,0:T(8,128)} %inv_ref.1, s32[1,64]{1,0:T(1,128)} %bitcast.7), custom_call_target="tpu_custom_call" | custom-call | tf_op jit(solution)/shard_map/pallas_call | solution.py:652
  61.6 0.8 %shard_map.78 = (f32[64,1024]{1,0:T(8,128)}, f32[64,1024]{1,0:T(8,128)}) custom-call(f32[64,1024]{1,0:T(8,128)S(1)} %get-tuple-element.4.sol_ref, f32[64,1024]{1,0:T(8,128)S(1)} %get-tuple-element.5.res_ref), custom_call_target="tpu_custom_call" | custom-call | tf_op jit(solution)/shard_map/pallas_call | solution.py:668
